TPU v7x, 512 devices: a whole 4x4x16 slice. The times are simulated.
512 devices in a mesh: dp: 4 (over x), cand: 32 (over z, core), tensor: 4 (over y).
Axes of the slice: x: 4, y: 4, z: 16, core: 2. Of those that a mesh axis runs over, the one named last changes fastest.
Arguments:
- context: bfloat16 [8, 4096, 3584], P('dp', 'cand', 'tensor'), may hold values from -12 to 12
- residual: bfloat16 [8, 4096, 3584], P('dp', ('cand', 'tensor')), may hold values from -36 to 36
- out_weight: bfloat16 [3584, 3584], P('cand', 'tensor'), may hold values from -0.09375 to 0.09375
- adapter_down: bfloat16 [3584, 16], P('tensor'), may hold values from -0.09375 to 0.09375
- adapter_up_weight: bfloat16 [16, 3584], replicated, may hold values from -1.5 to 1.5
- norm_gain: float32 [3584], replicated, may hold values from 0.5 to 1.5
- score_weight: float32 [3584], replicated, may hold values from -0.09375 to 0.09375
- teacher: bfloat16 [8, 4096, 4096], P('dp', 'cand', 'tensor'), may hold values from 0.019897461 to 0.9765625
- pair_mask: int32 [8, 4096, 4096], P('dp', 'cand', 'tensor'), may hold values from 0 to 1, as said below
- loss_scale: float32 [8], P('dp'), may hold values from 65536 to 262144
Outputs:
- context_grad: bfloat16 [8, 4096, 3584], P('dp', 'cand', 'tensor')
- residual_gradient: bfloat16 [8, 4096, 3584], P('dp', ('cand', 'tensor'))
- down_grad: float32 [3584, 16], P('tensor')
- up_weight_gradient: float32 [16, 3584], P(None, 'tensor')
- pair_loss: float32 [8], P('dp')
Inputs may be any that keep to these rules, and one draw needn't show every extreme that they name: pair_mask holds 0 or 1; with P = 32, every pair (i, j) whose group j // P lies 4096 / (2P) groups after i // P, counted round over the 4096 / P groups, is valid.
All inputs are finite; a program needn't handle non-finite values.
Results may differ from a plain program's by a relative error of at most 0.02.
Values may be sent and summed in bfloat16 or wider, within the bound.
No kernel may reach another device: no remote copies, remote signals or barrier semaphores. Data moves between devices by JAX's collectives and lax.ppermute only.
A program may use at most 64 MiB of HBM per device.

v0:
```python
import jax
import jax.numpy as jnp
from jax import lax
from jax.sharding import PartitionSpec as P

ADAPTER_SCALE = 0.5
epsilon = 1e-06
F32 = jnp.float32
BF16 = jnp.bfloat16


def gather_copies(x, axis):
    copies = jnp.broadcast_to(x[None], (lax.axis_size(axis),) + x.shape)
    return lax.all_to_all(copies, axis, 0, 0, tiled=True)


def on_device(
    context,
    residual,
    out_weight,
    adapter_down,
    adapter_up_weight,
    norm_gain,
    score_weight,
    teacher,
    pair_mask,
    loss_scale,
):
    queries, cand_rows, _ = context.shape
    width = residual.shape[2]
    cols = teacher.shape[2]
    tensor_count = lax.axis_size("tensor")
    cand_count = lax.axis_size("cand")
    share = cand_rows // tensor_count
    near = cols // cand_rows
    tensor_index = lax.axis_index("tensor")
    dp_index = lax.axis_index("dp")
    cand_index = lax.axis_index("cand")
    dp_count = lax.axis_size("dp")
    full_weight = lax.all_gather(out_weight, "cand", axis=0, tiled=True)
    low_terms = jnp.einsum("qch,hr->qcr", context, adapter_down, preferred_element_type=F32).astype(
        BF16
    )
    low_all = lax.all_gather(low_terms, "tensor", axis=0)
    adapter_in = jnp.sum(low_all.astype(F32), axis=0).astype(BF16)
    adapter_own = lax.dynamic_slice_in_dim(adapter_in, tensor_index * share, share, 1)
    lifted = jnp.einsum("qcr,rd->qcd", adapter_own, adapter_up_weight, preferred_element_type=F32)
    base = residual.astype(F32) + ADAPTER_SCALE * lifted
    mask_count = jnp.sum(pair_mask.astype(F32), axis=(1, 2))
    pairs = gather_copies(jnp.stack([pair_mask.astype(BF16), teacher]), "tensor")
    known = pairs[:, 0].astype(F32) * pairs[:, 1].astype(F32)
    row_known = jnp.sum(known, axis=(0, 3))
    col_known = jnp.sum(known, axis=2)
    full_weight, adapter_in, base, mask_count, pairs, row_known, col_known = (
        lax.optimization_barrier(
            (full_weight, adapter_in, base, mask_count, pairs, row_known, col_known)
        )
    )
    by_owner = jnp.swapaxes(context.reshape(queries, tensor_count, share, context.shape[2]), 0, 1)
    head_terms = jnp.einsum(
        "tqch,dh->tqcd", by_owner, full_weight, preferred_element_type=F32
    ).astype(BF16)
    head_terms = lax.all_to_all(head_terms, "tensor", 0, 0, tiled=True)
    hidden = (base + jnp.sum(head_terms.astype(F32), axis=0)).astype(BF16).astype(F32)
    inv_rms = lax.rsqrt(jnp.mean(hidden * hidden, axis=2) + epsilon)
    gain = norm_gain * score_weight
    dot = jnp.sum(hidden * gain, axis=2)
    scores = dot * inv_rms
    slant = inv_rms * inv_rms * dot / width
    unit = inv_rms[:, :, None] * (gain - hidden * slant[:, :, None])
    pairs, scores = lax.optimization_barrier((pairs, scores))
    valid = lax.optimization_barrier(pairs[:, 0])
    unit_sent, unit, scores = lax.optimization_barrier((unit.astype(BF16), unit, scores))
    unit_all = lax.all_gather(unit_sent, "tensor", axis=1, tiled=True)
    message = jnp.concatenate(
        [scores, jnp.broadcast_to(mask_count[:, None], (queries, 128 - share))], axis=1
    )
    message = gather_copies(message, ("cand", "tensor"))
    count = jnp.sum(message[:, :, share], axis=0)
    message = message[:, :, :share].reshape(cand_count, tensor_count, queries, share)
    own_scores = lax.dynamic_index_in_dim(message, cand_index, 0, keepdims=False)
    own_scores = jnp.swapaxes(own_scores, 0, 1).reshape(queries, cand_rows)
    message = message.reshape(tensor_count, near, tensor_count, queries, share)
    col_scores = jnp.moveaxis(message, 3, 1).reshape(tensor_count, queries, cols)
    margin = own_scores[None, :, :, None] - col_scores[:, :, None, :]
    chance = valid.astype(F32) * jax.nn.sigmoid(margin)
    row_sum = jnp.sum(chance, axis=(0, 3)) - row_known
    columns = jnp.sum(chance, axis=2) - col_known
    columns = columns.reshape(tensor_count, queries, near, cand_rows)
    columns = jnp.swapaxes(columns, 1, 2).reshape(cand_count, queries, cand_rows)
    columns, row_sum, own_late, col_late = lax.optimization_barrier(
        (columns, row_sum, own_scores, col_scores)
    )
    columns = lax.all_to_all(columns, "cand", 0, 0, tiled=True)
    margin = own_late[None, :, :, None] - col_late[:, :, None, :]
    total = (
        jnp.sum(valid.astype(F32) * jax.nn.softplus(margin), axis=(0, 2, 3))
        - jnp.sum(own_late * row_known, axis=1)
        + jnp.sum(col_late * col_known, axis=(0, 2))
    )
    adapter_unit = ADAPTER_SCALE * jnp.einsum(
        "qcd,rd->qcr", unit_all, adapter_up_weight, preferred_element_type=F32
    )
    context_unit = jnp.einsum(
        "qcd,dh->qch", unit_all, full_weight, preferred_element_type=F32
    ) + jnp.einsum(
        "qcr,hr->qch", adapter_unit.astype(BF16), adapter_down, preferred_element_type=F32
    )
    unit_block = lax.dynamic_slice_in_dim(
        unit_all, tensor_index * context.shape[2], context.shape[2], 2
    )
    columns, total, adapter_unit, context_unit, unit_block, count = lax.optimization_barrier(
        (columns, total, adapter_unit, context_unit, unit_block, count)
    )
    score_grad = (row_sum - jnp.sum(columns, axis=0)) * (loss_scale / count)[:, None]
    own_grad = lax.dynamic_slice_in_dim(score_grad, tensor_index * share, share, 1)
    grad_rows = (own_grad[:, :, None] * unit).astype(BF16)
    context_grad = (score_grad[:, :, None] * context_unit).astype(BF16)
    adapter_back = (score_grad[:, :, None] * adapter_unit).astype(BF16)
    down_local = jnp.einsum("qcr,qch->rh", adapter_back, context, preferred_element_type=F32)
    adapter_scaled = (score_grad[:, :, None] * adapter_in.astype(F32)).astype(BF16)
    up_local = ADAPTER_SCALE * jnp.einsum(
        "qcr,qcd->rd", adapter_scaled, unit_block, preferred_element_type=F32
    )
    rank = adapter_down.shape[1]
    flat = jnp.concatenate([down_local, up_local], axis=0)
    wide = flat.shape[1]
    segments = cand_count // near
    members = dp_count * near
    near_groups = [
        [d * cand_count + a * near + b for d in range(dp_count) for b in range(near)]
        for a in range(segments)
    ]
    far_groups = [[a * near + b for a in range(segments)] for b in range(near)]
    slots = lax.dynamic_update_slice_in_dim(
        jnp.zeros((1, 1, 128), F32), total[None, None, :], dp_index * queries, 2
    )
    tiles = flat.reshape(2 * rank // 8, 8, wide // 128, 128)
    tiles = jnp.swapaxes(tiles, 1, 2).reshape(-1, 8, 128)
    used = tiles.shape[0]
    height = -(-(used + 1) // members)
    slots = jnp.pad(slots, ((0, height * members - used - 1), (0, 7), (0, 0)))
    tiles = jnp.concatenate([tiles, slots]).reshape(members, 8 * height, 128)
    tiles = lax.all_to_all(tiles, ("dp", "cand"), 0, 0, axis_index_groups=near_groups, tiled=True)
    tiles = lax.psum(jnp.sum(tiles, axis=0), "cand", axis_index_groups=far_groups)
    tiles = jnp.broadcast_to(tiles[None], (members,) + tiles.shape)
    tiles = lax.all_to_all(
        tiles, ("dp", "cand"), 0, 0, axis_index_groups=near_groups, tiled=True
    ).reshape(-1, 8, 128)
    loss_sum = lax.dynamic_slice_in_dim(tiles[used, 0], dp_index * queries, queries, 0)
    pair_loss = loss_sum / count
    flat = tiles[:used].reshape(2 * rank // 8, wide // 128, 8, 128)
    flat = jnp.swapaxes(flat, 1, 2).reshape(2 * rank, wide)
    down_grad = flat[:rank].T
    up_weight_gradient = flat[rank:]
    return (context_grad, grad_rows, down_grad, up_weight_gradient, pair_loss)


def solution(mesh):
    in_specs = (
        P("dp", "cand", "tensor"),
        P("dp", ("cand", "tensor"), None),
        P("cand", "tensor"),
        P("tensor", None),
        P(),
        P(),
        P(),
        P("dp", "cand", "tensor"),
        P("dp", "cand", "tensor"),
        P("dp"),
    )
    out_specs = (
        P("dp", "cand", "tensor"),
        P("dp", ("cand", "tensor"), None),
        P("tensor", None),
        P(None, "tensor"),
        P("dp"),
    )
    return jax.shard_map(
        on_device, mesh=mesh, in_specs=in_specs, out_specs=out_specs, check_vma=False
    )
```

profile of v0, /device:TPU:1, one launch (start us, length us, event | category | flops | bytes accessed | tf_op | source)
XLA Modules:
  0.0 228.8 jit_solution(7035708157234387548)
XLA Ops:
  7.2 0.7 all-gather.4.cloned.1.call-update
  7.9 1.3 convert_bitcast_fusion
  9.2 1.1 pad_maximum_fusion
  10.4 2.6 %broadcast_in_dim.12 = bf16[4,2,2,128,1024]{4,3,2,1,0:T(8,128)(2,1)} broadcast(bf16[2,2,128,1024]{3,2,1,0:T(8,128)(2,1)S(1)} %pad_maximum_fusion), dimensions={1,2,3,4} | broadcast | bytes 5242880 | tf_op jit(solution)/shard_map/broadcast_in_dim | solution.py:13
  13.0 5.2 %all-to-all-start = ((bf16[4,2,2,128,1024]{4,3,2,1,0:T(8,128)(2,1)}), bf16[4,2,2,128,1024]{4,3,2,1,0:T(8,128)(2,1)}, u32[]{:S(2)}, u32[]{:S(2)}) async-start(bf16[4,2,2,128,1024]{4,3,2,1,0:T(8,128)(2,1)} %broadcast_in_dim.12), calls=%async_computation | async-start | bytes 8388608 | tf_op jit(solution)/shard_map/all_to_all | solution.py:14
  18.4 47.8 %all-gather = bf16[8,128,16]{1,2,0:T(8,128)(2,1)S(1)} all-gather(bf16[2,128,16]{1,2,0:T(8,128)(2,1)S(1)} %convolution_convert_fusion), channel_id=2, replica_groups=mesh['dp'=4,'cand'=32,'tensor'=4] {'tensor'}, dimensions={0}, use_global_device_ids=true | all-gather | bytes 40960 | tf_op jit(solution)/shard_map/all_gather | solution.py:44
  66.8 3.3 %fusion.16 = (f32[4,2,1024]{2,1,0:T(2,128)S(1)}, f32[2,128]{1,0:T(2,128)S(1)}) fusion(bf16[4,2,2,128,1024]{4,3,2,1,0:T(8,128)(2,1)} %all-to-all-done), kind=kLoop, calls=%fused_computation.19 | loop fusion | flops 5234432 | bytes 4228096 | tf_op jit(solution)/shard_map/reduce_sum | solution.py:53
  70.0 22.9 %all-gather.4.cloned.1.call-done = bf16[3584,896]{1,0:T(8,128)(2,1)} async-done(((bf16[112,896]{1,0:T(8,128)(2,1)}), bf16[3584,896]{1,0:T(8,128)(2,1)}) %all-gather.4.cloned.1.call-update) | async-done | bytes 6422544 | tf_op jit(solution)/shard_map/all_gather | solution.py:40
  93.0 6.2 %fusion.7 = bf16[4,2,32,3584]{3,2,1,0:T(8,128)(2,1)} fusion(bf16[3584,896]{1,0:T(8,128)(2,1)} %all-gather.4.cloned.1.call-done, bf16[2,4,32,896]{3,2,1,0:T(8,128)(2,1)S(1)} %bitcast.80), kind=kOutput, calls=%fused_computation.10 | convolution fusion | flops 1645084672 | bytes 8716288 | tf_op jit(solution)/shard_map/tqch,dh->tqcd/dot_general | solution.py:60
  99.1 4.1 %all-to-all-start.1 = ((bf16[4,2,32,3584]{3,2,1,0:T(8,128)(2,1)}), bf16[4,2,32,3584]{3,2,1,0:T(8,128)(2,1)S(1)}, u32[]{:S(2)}, u32[]{:S(2)}) async-start(bf16[4,2,32,3584]{3,2,1,0:T(8,128)(2,1)} %fusion.7), calls=%async_computation.1 | async-start | bytes 3670016 | tf_op jit(solution)/shard_map/all_to_all | solution.py:63
  103.2 23.1 %all-to-all-done.1 = bf16[4,2,32,3584]{3,2,1,0:T(8,128)(2,1)S(1)} async-done(((bf16[4,2,32,3584]{3,2,1,0:T(8,128)(2,1)}), bf16[4,2,32,3584]{3,2,1,0:T(8,128)(2,1)S(1)}, u32[]{:S(2)}, u32[]{:S(2)}) %all-to-all-start.1) | async-done | bytes 1835040 | tf_op jit(solution)/shard_map/all_to_all | solution.py:63
  126.9 1.0 fusion.24
  128.0 0.7 broadcast_in_dim.14
  128.7 10.7 %all-to-all-start.2 = ((f32[128,2,128]{2,1,0:T(2,128)}), f32[128,2,128]{2,1,0:T(2,128)S(1)}, u32[]{:S(2)}, u32[]{:S(2)}) async-start(f32[128,2,128]{2,1,0:T(2,128)} %broadcast_in_dim.14), calls=%async_computation.2 | async-start | bytes 262144 | tf_op jit(solution)/shard_map/all_to_all | solution.py:14
  139.4 2.0 slice_bitcast_fusion
  141.4 16.1 %all-to-all-done.2 = f32[128,2,128]{2,1,0:T(2,128)S(1)} async-done(((f32[128,2,128]{2,1,0:T(2,128)}), f32[128,2,128]{2,1,0:T(2,128)S(1)}, u32[]{:S(2)}, u32[]{:S(2)}) %all-to-all-start.2) | async-done | bytes 131104 | tf_op jit(solution)/shard_map/all_to_all | solution.py:14
  157.8 1.8 fusion.18
  159.7 0.6 copy.35
  160.3 3.8 %all-to-all-start.3 = ((f32[32,2,128]{2,1,0:T(2,128)}), f32[32,2,128]{2,1,0:T(2,128)S(1)}, u32[]{:S(2)}, u32[]{:S(2)}) async-start(f32[32,2,128]{2,1,0:T(2,128)} %copy.35), calls=%async_computation.3 | async-start | bytes 65536 | tf_op jit(solution)/shard_map/all_to_all | solution.py:94
  164.8 2.9 %fusion.11 = f32[2]{0:T(128)S(1)} fusion(bf16[4,2,128,1024]{3,2,1,0:T(8,128)(2,1)S(1)} %slice_bitcast_fusion, f32[4,2,1024]{2,1,0:T(2,128)S(1)} %copy.37, f32[2,128]{1,0:T(2,128)S(1)} %sub.49), kind=kLoop, calls=%fused_computation.13 | loop fusion | flops 10485758 | bytes 2130952 | tf_op jit(solution)/shard_map/reduce_sum | solution.py:97
  167.6 5.6 %fusion.2 = f32[2,128,896]{2,1,0:T(8,128)S(1)} fusion(bf16[2,128,3584]{2,1,0:T(8,128)(2,1)} %all-gather.6.cloned.1.call-done, bf16[3584,896]{1,0:T(8,128)(2,1)} %all-gather.4.cloned.1.call-done), kind=kOutput, calls=%fused_computation.5 | convolution fusion | flops 1644167168 | bytes 9175040 | tf_op jit(solution)/shard_map/qcd,dh->qch/dot_general | solution.py:104
  174.2 1.4 all-to-all-done.3
  176.3 0.7 select_maximum_fusion
  177.0 5.9 %all-to-all-start.4 = ((f32[32,8,128]{2,1,0:T(8,128)}), f32[32,8,128]{2,1,0:T(8,128)S(1)}, u32[]{:S(2)}, u32[]{:S(2)}) async-start(f32[32,8,128]{2,1,0:T(8,128)} %select_maximum_fusion), calls=%async_computation.4 | async-start | bytes 262144 | tf_op jit(solution)/shard_map/all_to_all | solution.py:144
  182.9 8.6 %all-to-all-done.4 = f32[32,8,128]{2,1,0:T(8,128)S(1)} async-done(((f32[32,8,128]{2,1,0:T(8,128)}), f32[32,8,128]{2,1,0:T(8,128)S(1)}, u32[]{:S(2)}, u32[]{:S(2)}) %all-to-all-start.4) | async-done | bytes 131104 | tf_op jit(solution)/shard_map/all_to_all | solution.py:144
  191.6 13.8 %psum.7 = f32[8,128]{1,0:T(8,128)S(1)} all-reduce(f32[8,128]{1,0:T(8,128)S(1)} %reduce_sum.152), channel_id=1, replica_groups={{0,32,64,96},{4,36,68,100},{8,40,72,104},{12,44,76,108},{16,48,80,112},..., use_global_device_ids=true, to_apply=%region_15.16 | all-reduce | flops 1024 | bytes 8192 | tf_op jit(solution)/shard_map/psum | solution.py:145
  205.3 0.6 broadcast_in_dim.17
  206.0 5.9 %all-to-all-start.5 = ((f32[32,8,128]{2,1,0:T(8,128)}), f32[32,8,128]{2,1,0:T(8,128)S(1)}, u32[]{:S(2)}, u32[]{:S(2)}) async-start(f32[32,8,128]{2,1,0:T(8,128)} %broadcast_in_dim.17), calls=%async_computation.5 | async-start | bytes 262144 | tf_op jit(solution)/shard_map/all_to_all | solution.py:147
  211.9 0.9 multiply_convert_fusion
  212.8 0.9 multiply_convert_fusion.1
  213.7 7.0 %all-to-all-done.5 = f32[32,8,128]{2,1,0:T(8,128)S(1)} async-done(((f32[32,8,128]{2,1,0:T(8,128)}), f32[32,8,128]{2,1,0:T(8,128)S(1)}, u32[]{:S(2)}, u32[]{:S(2)}) %all-to-all-start.5) | async-done | bytes 131104 | tf_op jit(solution)/shard_map/all_to_all | solution.py:147
  221.3 0.6 slice_bitcast_fusion.1
  (64 shorter events, 4.9 us)
Async XLA Ops:
  7.2 59.2 %copy-start = (bf16[16,3584]{1,0:T(8,128)(2,1)S(1)}, bf16[16,3584]{1,0:T(8,128)(2,1)}, u32[]{:S(2)}) copy-start(bf16[16,3584]{1,0:T(8,128)(2,1)} %param.14) | copy-start | bytes 344068
  7.2 85.8 %all-gather.4.cloned.1.call-start = ((), (), s32[]{:S(2)}) async-start(), calls=%async_computation.6 | async-start | bytes 6623232 | tf_op jit(solution)/shard_map/all_gather | solution.py:40
  13.0 5.2 %copy-start.3 = (bf16[2,128,896]{2,1,0:T(8,128)(2,1)S(1)}, bf16[2,128,896]{2,1,0:T(8,128)(2,1)}, u32[]{:S(2)}) copy-start(bf16[2,128,896]{2,1,0:T(8,128)(2,1)} %param.10) | copy-start | bytes 1376260
  13.0 5.2 %copy-start.6 = (bf16[896,16]{0,1:T(8,128)(2,1)S(1)}, bf16[896,16]{0,1:T(8,128)(2,1)}, u32[]{:S(2)}) copy-start(bf16[896,16]{0,1:T(8,128)(2,1)} %param.13) | copy-start | bytes 86020
  13.0 53.1 %copy-start.1 = (s32[2,128,1024]{2,1,0:T(8,128)S(1)}, s32[2,128,1024]{2,1,0:T(8,128)}, u32[]{:S(2)}) copy-start(s32[2,128,1024]{2,1,0:T(8,128)} %param.18) | copy-start | bytes 3145732
  13.0 53.4 %copy-start.5 = (bf16[2,32,3584]{2,1,0:T(8,128)(2,1)S(1)}, bf16[2,32,3584]{2,1,0:T(8,128)(2,1)}, u32[]{:S(2)}) copy-start(bf16[2,32,3584]{2,1,0:T(8,128)(2,1)} %param.11) | copy-start | bytes 1376260
  13.0 53.8 %all-to-all-start = ((bf16[4,2,2,128,1024]{4,3,2,1,0:T(8,128)(2,1)}), bf16[4,2,2,128,1024]{4,3,2,1,0:T(8,128)(2,1)}, u32[]{:S(2)}, u32[]{:S(2)}) async-start(bf16[4,2,2,128,1024]{4,3,2,1,0:T(8,128)(2,1)} %broadcast_in_dim.12), calls=%async_computation | async-start | bytes 8388608 | tf_op jit(solution)/shard_map/all_to_all | solution.py:14
  93.0 10.2 %copy-start.7 = (f32[3584]{0:T(1024)S(1)}, f32[3584]{0:T(1024)}, u32[]{:S(2)}) copy-start(f32[3584]{0:T(1024)} %param.15) | copy-start | bytes 43012
  93.0 10.2 %copy-start.8 = (f32[3584]{0:T(1024)S(1)}, f32[3584]{0:T(1024)}, u32[]{:S(2)}) copy-start(f32[3584]{0:T(1024)} %param.16) | copy-start | bytes 43012
  99.1 27.1 %all-to-all-start.1 = ((bf16[4,2,32,3584]{3,2,1,0:T(8,128)(2,1)}), bf16[4,2,32,3584]{3,2,1,0:T(8,128)(2,1)S(1)}, u32[]{:S(2)}, u32[]{:S(2)}) async-start(bf16[4,2,32,3584]{3,2,1,0:T(8,128)(2,1)} %fusion.7), calls=%async_computation.1 | async-start | bytes 3670016 | tf_op jit(solution)/shard_map/all_to_all | solution.py:63
  103.2 64.4 %all-gather.6.cloned.1.call-start = ((), (), s32[]{:S(2)}) async-start(), calls=%async_computation.7 | async-start | bytes 2293760 | tf_op jit(solution)/shard_map/all_gather | solution.py:74
  128.7 28.8 %all-to-all-start.2 = ((f32[128,2,128]{2,1,0:T(2,128)}), f32[128,2,128]{2,1,0:T(2,128)S(1)}, u32[]{:S(2)}, u32[]{:S(2)}) async-start(f32[128,2,128]{2,1,0:T(2,128)} %broadcast_in_dim.14), calls=%async_computation.2 | async-start | bytes 262144 | tf_op jit(solution)/shard_map/all_to_all | solution.py:14
  160.3 15.3 %all-to-all-start.3 = ((f32[32,2,128]{2,1,0:T(2,128)}), f32[32,2,128]{2,1,0:T(2,128)S(1)}, u32[]{:S(2)}, u32[]{:S(2)}) async-start(f32[32,2,128]{2,1,0:T(2,128)} %copy.35), calls=%async_computation.3 | async-start | bytes 65536 | tf_op jit(solution)/shard_map/all_to_all | solution.py:94
  167.6 5.6 %copy-start.2 = (bf16[2,128,3584]{2,1,0:T(8,128)(2,1)S(1)}, bf16[2,128,3584]{2,1,0:T(8,128)(2,1)}, u32[]{:S(2)}) copy-start(bf16[2,128,3584]{2,1,0:T(8,128)(2,1)} %all-gather.6.cloned.1.call-done) | copy-start | bytes 5505028
  173.2 2.4 %copy-start.9 = (f32[2]{0:T(128)S(1)}, f32[2]{0:T(128)}, u32[]{:S(2)}) copy-start(f32[2]{0:T(128)} %param.19) | copy-start | bytes 28
  173.2 2.5 %copy-start.4 = (bf16[2,128,896]{2,1,0:T(8,128)(2,1)S(1)}, bf16[2,128,896]{2,1,0:T(8,128)(2,1)}, u32[]{:S(2)}) copy-start(bf16[2,128,896]{2,1,0:T(8,128)(2,1)} %param.10) | copy-start | bytes 1376260
  177.0 14.6 %all-to-all-start.4 = ((f32[32,8,128]{2,1,0:T(8,128)}), f32[32,8,128]{2,1,0:T(8,128)S(1)}, u32[]{:S(2)}, u32[]{:S(2)}) async-start(f32[32,8,128]{2,1,0:T(8,128)} %select_maximum_fusion), calls=%async_computation.4 | async-start | bytes 262144 | tf_op jit(solution)/shard_map/all_to_all | solution.py:144
  206.0 14.8 %all-to-all-start.5 = ((f32[32,8,128]{2,1,0:T(8,128)}), f32[32,8,128]{2,1,0:T(8,128)S(1)}, u32[]{:S(2)}, u32[]{:S(2)}) async-start(f32[32,8,128]{2,1,0:T(8,128)} %broadcast_in_dim.17), calls=%async_computation.5 | async-start | bytes 262144 | tf_op jit(solution)/shard_map/all_to_all | solution.py:147
Sparse Core Ops, SparseCore 0:
  10.1 82.7 all-gather.3
  128.0 32.9 all-gather.5
where the time goes:
time: 229 us
  waiting for transfers between devices  79.9 us (35%)
  blocking collectives  61.5 us (27%)
  starting transfers between devices  35.5 us (16%)
  other arithmetic  16.1 us (7%)
  between operations  14.3 us (6%)
  matrix products  13.6 us (6%)
  local copies, waits for them, and re-layouts  7.95 us (3%)
    all_gather x1, blocking collectives, on_device(): low_all = lax.all_gather(low_terms, 'tensor', axis=0)  47.8 us
    all_to_all x1, waiting for transfers between devices, on_device(): head_terms = lax.all_to_all(head_terms, 'tensor', 0, 0, tiled=True)  23.1 us
    all_gather x1, waiting for transfers between devices, on_device(): full_weight = lax.all_gather(out_weight, 'cand', axis=0, tiled=True)  22.9 us
    all_to_all x2, waiting for transfers between devices, gather_copies(): return lax.all_to_all(copies, axis, 0, 0, tiled=True)  16.1 us
    all_to_all x2, starting transfers between devices, gather_copies(): return lax.all_to_all(copies, axis, 0, 0, tiled=True)  15.8 us
    all_to_all x2, waiting for transfers between devices, on_device(): lax.all_to_all(tiles, ('dp', 'cand'), 0, 0, axis_index_groups=near_groups...  15.7 us
    psum x1, blocking collectives, on_device(): lax.psum(jnp.sum(tiles, axis=0), 'cand', axis_index_groups=far_groups)  13.8 us
    all_to_all x2, starting transfers between devices, on_device(): lax.all_to_all(tiles, ('dp', 'cand'), 0, 0, axis_index_groups=near_groups...  11.8 us
  transfers between devices with their start and end apart: 8, of which 6 were waited for; matrix products, arithmetic and copies ran while one was open for 12% of the time, Pallas kernels for 0%

commit v1 on v0

--- a/solution.py
+++ b/solution.py
@@ -37,7 +37,9 @@
     dp_index = lax.axis_index("dp")
     cand_index = lax.axis_index("cand")
     dp_count = lax.axis_size("dp")
-    full_weight = lax.all_gather(out_weight, "cand", axis=0, tiled=True)
+    full_weight = jnp.concatenate(
+        lax.all_to_all(jnp.stack([out_weight] * lax.axis_size("cand")), "cand", 0, 0), axis=0
+    )
     low_terms = jnp.einsum("qch,hr->qcr", context, adapter_down, preferred_element_type=F32).astype(
         BF16
     )

time: 229 us -> 503 us (2.20)
  waiting for transfers between devices: 79.9 us -> 322 us
  starting transfers between devices: 35.5 us -> 54.3 us
  blocking collectives: 61.5 us -> 71 us
    all_to_all x0 -> x1, waiting for transfers between devices: none -> 267 us  [on_device(): lax.all_to_all(jnp.stack([out_weight] * lax.axis_size('cand')), 'cand', 0...]
    all_to_all x0 -> x1, blocking collectives: none -> 48.1 us  [gather_copies(): return lax.all_to_all(copies, axis, 0, 0, tiled=True)]
    all_gather x1, blocking collectives: 47.8 us -> 9.07 us  [on_device(): low_all = lax.all_gather(low_terms, 'tensor', axis=0)]
    all_gather x1 -> x0, waiting for transfers between devices: 22.9 us -> none  [on_device(): full_weight = lax.all_gather(out_weight, 'cand', axis=0, tiled=True)]
    all_to_all x0 -> x1, starting transfers between devices: none -> 22.1 us  [on_device(): lax.all_to_all(jnp.stack([out_weight] * lax.axis_size('cand')), 'cand', 0...]
    all_to_all x2 -> x1, starting transfers between devices: 15.8 us -> 11.5 us  [gather_copies(): return lax.all_to_all(copies, axis, 0, 0, tiled=True)]
    all_to_all x2 -> x1, waiting for transfers between devices: 16.1 us -> 16.1 us  [gather_copies(): return lax.all_to_all(copies, axis, 0, 0, tiled=True)]
  transfers between devices with their start and end apart: 8 -> 7, of which waited for: 6 -> 5; matrix products, arithmetic and copies ran while one was open for 12% -> 5% of each run, Pallas kernels for 0% -> 0%
where the time goes in v1:
time: 503 us
  waiting for transfers between devices  322 us (64%)
  blocking collectives  71 us (14%)
  starting transfers between devices  54.3 us (11%)
  other arithmetic  16.1 us (3%)
  matrix products  15 us (3%)
  between operations  14.4 us (3%)
  local copies, waits for them, and re-layouts  10 us (2%)
    all_to_all x1, waiting for transfers between devices, on_device(): lax.all_to_all(jnp.stack([out_weight] * lax.axis_size('cand')), 'cand', 0...  267 us
    all_to_all x1, blocking collectives, gather_copies(): return lax.all_to_all(copies, axis, 0, 0, tiled=True)  48.1 us
    all_to_all x1, waiting for transfers between devices, on_device(): head_terms = lax.all_to_all(head_terms, 'tensor', 0, 0, tiled=True)  23 us
    all_to_all x1, starting transfers between devices, on_device(): lax.all_to_all(jnp.stack([out_weight] * lax.axis_size('cand')), 'cand', 0...  22.1 us
    all_to_all x1, waiting for transfers between devices, gather_copies(): return lax.all_to_all(copies, axis, 0, 0, tiled=True)  16.1 us
    all_to_all x2, waiting for transfers between devices, on_device(): lax.all_to_all(tiles, ('dp', 'cand'), 0, 0, axis_index_groups=near_groups...  15.7 us
    psum x1, blocking collectives, on_device(): lax.psum(jnp.sum(tiles, axis=0), 'cand', axis_index_groups=far_groups)  13.8 us
    all_to_all x2, starting transfers between devices, on_device(): lax.all_to_all(tiles, ('dp', 'cand'), 0, 0, axis_index_groups=near_groups...  13.2 us
  transfers between devices with their start and end apart: 7, of which 5 were waited for; matrix products, arithmetic and copies ran while one was open for 5% of the time, Pallas kernels for 0%

profile of v1, /device:TPU:1, one launch (start us, length us, event | category | flops | bytes accessed | tf_op | source)
XLA Modules:
  0.0 502.5 jit_solution(17033316855669320370)
XLA Ops:
  7.2 1.3 convert_bitcast_fusion
  8.5 1.1 pad_maximum_fusion
  10.2 48.1 %all_to_all.35 = bf16[4,2,2,128,1024]{4,3,2,1,0:T(8,128)(2,1)} all-to-all(bf16[4,2,2,128,1024]{4,3,2,1,0:T(8,128)(2,1)S(1)} %broadcast_in_dim.12), channel_id=1, replica_groups=mesh['dp'=4,'cand'=32,'tensor'=4] {'tensor'}, dimensions={0} | all-to-all | bytes 8388608 | tf_op jit(solution)/shard_map/all_to_all | solution.py:14
  58.4 3.2 stack.8
  61.5 22.1 %all-to-all-start = ((bf16[32,112,896]{2,1,0:T(8,128)(2,1)}), bf16[32,112,896]{2,1,0:T(8,128)(2,1)}, u32[]{:S(2)}, u32[]{:S(2)}) async-start(bf16[32,112,896]{2,1,0:T(8,128)(2,1)} %stack.8), calls=%async_computation | async-start | bytes 12845056 | tf_op jit(solution)/shard_map/all_to_all | solution.py:41
  83.9 9.1 %all-gather = bf16[8,128,16]{1,2,0:T(8,128)(2,1)S(1)} all-gather(bf16[2,128,16]{1,2,0:T(8,128)(2,1)S(1)} %convolution_convert_fusion), channel_id=2, replica_groups=mesh['dp'=4,'cand'=32,'tensor'=4] {'tensor'}, dimensions={0}, use_global_device_ids=true | all-gather | bytes 40960 | tf_op jit(solution)/shard_map/all_gather | solution.py:46
  93.6 3.2 fusion.16
  96.8 267.0 %all-to-all-done = bf16[32,112,896]{2,1,0:T(8,128)(2,1)} async-done(((bf16[32,112,896]{2,1,0:T(8,128)(2,1)}), bf16[32,112,896]{2,1,0:T(8,128)(2,1)}, u32[]{:S(2)}, u32[]{:S(2)}) %all-to-all-start) | async-done | bytes 6422560 | tf_op jit(solution)/shard_map/all_to_all | solution.py:41
  363.8 6.2 %fusion.7 = bf16[4,2,32,3584]{3,2,1,0:T(8,128)(2,1)} fusion(bf16[3584,896]{1,0:T(8,128)(2,1)} %bitcast, bf16[2,4,32,896]{3,2,1,0:T(8,128)(2,1)S(1)} %bitcast.81), kind=kOutput, calls=%fused_computation.10 | convolution fusion | flops 1645084672 | bytes 8716288 | tf_op jit(solution)/shard_map/tqch,dh->tqcd/dot_general | solution.py:62
  370.0 3.6 all-to-all-start.2
  373.6 23.0 %all-to-all-done.2 = bf16[4,2,32,3584]{3,2,1,0:T(8,128)(2,1)S(1)} async-done(((bf16[4,2,32,3584]{3,2,1,0:T(8,128)(2,1)}), bf16[4,2,32,3584]{3,2,1,0:T(8,128)(2,1)S(1)}, u32[]{:S(2)}, u32[]{:S(2)}) %all-to-all-start.2) | async-done | bytes 1835040 | tf_op jit(solution)/shard_map/all_to_all | solution.py:65
  397.2 1.0 fusion.24
  398.4 0.7 broadcast_in_dim.14
  399.1 11.5 %all-to-all-start.3 = ((f32[128,2,128]{2,1,0:T(2,128)}), f32[128,2,128]{2,1,0:T(2,128)S(1)}, u32[]{:S(2)}, u32[]{:S(2)}) async-start(f32[128,2,128]{2,1,0:T(2,128)} %broadcast_in_dim.14), calls=%async_computation.3 | async-start | bytes 262144 | tf_op jit(solution)/shard_map/all_to_all | solution.py:14
  410.6 2.0 slice_bitcast_fusion
  412.6 16.1 %all-to-all-done.3 = f32[128,2,128]{2,1,0:T(2,128)S(1)} async-done(((f32[128,2,128]{2,1,0:T(2,128)}), f32[128,2,128]{2,1,0:T(2,128)S(1)}, u32[]{:S(2)}, u32[]{:S(2)}) %all-to-all-start.3) | async-done | bytes 131104 | tf_op jit(solution)/shard_map/all_to_all | solution.py:14
  429.1 1.8 fusion.18
  431.6 3.8 all-to-all-start.4
  436.0 2.9 fusion.11
  438.9 2.1 convolution_multiply_fusion.1
  441.0 5.5 %fusion.2 = f32[2,128,896]{2,1,0:T(8,128)S(1)} fusion(bf16[2,128,3584]{2,1,0:T(8,128)(2,1)} %all-gather.3.cloned.1.call-done, bf16[3584,896]{1,0:T(8,128)(2,1)} %bitcast), kind=kOutput, calls=%fused_computation.5 | convolution fusion | flops 1644167168 | bytes 9175040 | tf_op jit(solution)/shard_map/qcd,dh->qch/dot_general | solution.py:106
  446.8 1.1 constant_dynamic-slice_fusion.2
  448.6 0.7 select_maximum_fusion
  449.2 7.3 %all-to-all-start.5 = ((f32[32,8,128]{2,1,0:T(8,128)}), f32[32,8,128]{2,1,0:T(8,128)S(1)}, u32[]{:S(2)}, u32[]{:S(2)}) async-start(f32[32,8,128]{2,1,0:T(8,128)} %select_maximum_fusion), calls=%async_computation.5 | async-start | bytes 262144 | tf_op jit(solution)/shard_map/all_to_all | solution.py:146
  456.6 8.6 %all-to-all-done.5 = f32[32,8,128]{2,1,0:T(8,128)S(1)} async-done(((f32[32,8,128]{2,1,0:T(8,128)}), f32[32,8,128]{2,1,0:T(8,128)S(1)}, u32[]{:S(2)}, u32[]{:S(2)}) %all-to-all-start.5) | async-done | bytes 131104 | tf_op jit(solution)/shard_map/all_to_all | solution.py:146
  465.2 13.8 %psum.7 = f32[8,128]{1,0:T(8,128)S(1)} all-reduce(f32[8,128]{1,0:T(8,128)S(1)} %reduce_sum.152), channel_id=1, replica_groups={{0,32,64,96},{4,36,68,100},{8,40,72,104},{12,44,76,108},{16,48,80,112},..., use_global_device_ids=true, to_apply=%region_15.16 | all-reduce | flops 1024 | bytes 8192 | tf_op jit(solution)/shard_map/psum | solution.py:147
  479.0 0.6 broadcast_in_dim.17
  479.7 5.9 %all-to-all-start.6 = ((f32[32,8,128]{2,1,0:T(8,128)}), f32[32,8,128]{2,1,0:T(8,128)S(1)}, u32[]{:S(2)}, u32[]{:S(2)}) async-start(f32[32,8,128]{2,1,0:T(8,128)} %broadcast_in_dim.17), calls=%async_computation.6 | async-start | bytes 262144 | tf_op jit(solution)/shard_map/all_to_all | solution.py:149
  485.6 0.9 multiply_convert_fusion
  486.5 0.9 multiply_convert_fusion.1
  487.4 7.0 %all-to-all-done.6 = f32[32,8,128]{2,1,0:T(8,128)S(1)} async-done(((f32[32,8,128]{2,1,0:T(8,128)}), f32[32,8,128]{2,1,0:T(8,128)S(1)}, u32[]{:S(2)}, u32[]{:S(2)}) %all-to-all-start.6) | async-done | bytes 131104 | tf_op jit(solution)/shard_map/all_to_all | solution.py:149
  494.4 0.6 slice_bitcast_fusion.1
  (63 shorter events, 5.4 us)
Async XLA Ops:
  7.2 86.0 %copy-start = (bf16[16,3584]{1,0:T(8,128)(2,1)S(1)}, bf16[16,3584]{1,0:T(8,128)(2,1)}, u32[]{:S(2)}) copy-start(bf16[16,3584]{1,0:T(8,128)(2,1)} %param.14) | copy-start | bytes 344068
  10.2 48.2 %copy-start.5 = (bf16[112,896]{1,0:T(8,128)(2,1)S(1)}, bf16[112,896]{1,0:T(8,128)(2,1)}, u32[]{:S(2)}) copy-start(bf16[112,896]{1,0:T(8,128)(2,1)} %param.12) | copy-start | bytes 602116
  61.5 22.1 %copy-start.2 = (bf16[2,128,896]{2,1,0:T(8,128)(2,1)S(1)}, bf16[2,128,896]{2,1,0:T(8,128)(2,1)}, u32[]{:S(2)}) copy-start(bf16[2,128,896]{2,1,0:T(8,128)(2,1)} %param.10) | copy-start | bytes 1376260
  61.5 22.1 %copy-start.6 = (bf16[896,16]{0,1:T(8,128)(2,1)S(1)}, bf16[896,16]{0,1:T(8,128)(2,1)}, u32[]{:S(2)}) copy-start(bf16[896,16]{0,1:T(8,128)(2,1)} %param.13) | copy-start | bytes 86020
  61.5 31.4 %copy-start.1 = (s32[2,128,1024]{2,1,0:T(8,128)S(1)}, s32[2,128,1024]{2,1,0:T(8,128)}, u32[]{:S(2)}) copy-start(s32[2,128,1024]{2,1,0:T(8,128)} %param.18) | copy-start | bytes 3145732
  61.5 31.7 %copy-start.4 = (bf16[2,32,3584]{2,1,0:T(8,128)(2,1)S(1)}, bf16[2,32,3584]{2,1,0:T(8,128)(2,1)}, u32[]{:S(2)}) copy-start(bf16[2,32,3584]{2,1,0:T(8,128)(2,1)} %param.11) | copy-start | bytes 1376260
  61.5 302.2 %all-to-all-start = ((bf16[32,112,896]{2,1,0:T(8,128)(2,1)}), bf16[32,112,896]{2,1,0:T(8,128)(2,1)}, u32[]{:S(2)}, u32[]{:S(2)}) async-start(bf16[32,112,896]{2,1,0:T(8,128)(2,1)} %stack.8), calls=%async_computation | async-start | bytes 12845056 | tf_op jit(solution)/shard_map/all_to_all | solution.py:41
  363.8 9.8 %copy-start.7 = (f32[3584]{0:T(1024)S(1)}, f32[3584]{0:T(1024)}, u32[]{:S(2)}) copy-start(f32[3584]{0:T(1024)} %param.15) | copy-start | bytes 43012
  363.8 9.8 %copy-start.8 = (f32[3584]{0:T(1024)S(1)}, f32[3584]{0:T(1024)}, u32[]{:S(2)}) copy-start(f32[3584]{0:T(1024)} %param.16) | copy-start | bytes 43012
  370.0 26.7 %all-to-all-start.2 = ((bf16[4,2,32,3584]{3,2,1,0:T(8,128)(2,1)}), bf16[4,2,32,3584]{3,2,1,0:T(8,128)(2,1)S(1)}, u32[]{:S(2)}, u32[]{:S(2)}) async-start(bf16[4,2,32,3584]{3,2,1,0:T(8,128)(2,1)} %fusion.7), calls=%async_computation.2 | async-start | bytes 3670016 | tf_op jit(solution)/shard_map/all_to_all | solution.py:65
  373.6 65.3 %all-gather.3.cloned.1.call-start = ((), (), s32[]{:S(2)}) async-start(), calls=%async_computation.7 | async-start | bytes 2293760 | tf_op jit(solution)/shard_map/all_gather | solution.py:76
  399.1 29.7 %all-to-all-start.3 = ((f32[128,2,128]{2,1,0:T(2,128)}), f32[128,2,128]{2,1,0:T(2,128)S(1)}, u32[]{:S(2)}, u32[]{:S(2)}) async-start(f32[128,2,128]{2,1,0:T(2,128)} %broadcast_in_dim.14), calls=%async_computation.3 | async-start | bytes 262144 | tf_op jit(solution)/shard_map/all_to_all | solution.py:14
  431.6 16.3 %all-to-all-start.4 = ((f32[32,2,128]{2,1,0:T(2,128)}), f32[32,2,128]{2,1,0:T(2,128)S(1)}, u32[]{:S(2)}, u32[]{:S(2)}) async-start(f32[32,2,128]{2,1,0:T(2,128)} %copy.35), calls=%async_computation.4 | async-start | bytes 65536 | tf_op jit(solution)/shard_map/all_to_all | solution.py:96
  440.9 7.0 %copy-start.9 = (f32[2]{0:T(128)S(1)}, f32[2]{0:T(128)}, u32[]{:S(2)}) copy-start(f32[2]{0:T(128)} %param.19) | copy-start | bytes 28
  440.9 7.1 %copy-start.3 = (bf16[2,128,896]{2,1,0:T(8,128)(2,1)S(1)}, bf16[2,128,896]{2,1,0:T(8,128)(2,1)}, u32[]{:S(2)}) copy-start(bf16[2,128,896]{2,1,0:T(8,128)(2,1)} %param.10) | copy-start | bytes 1376260
  449.2 16.0 %all-to-all-start.5 = ((f32[32,8,128]{2,1,0:T(8,128)}), f32[32,8,128]{2,1,0:T(8,128)S(1)}, u32[]{:S(2)}, u32[]{:S(2)}) async-start(f32[32,8,128]{2,1,0:T(8,128)} %select_maximum_fusion), calls=%async_computation.5 | async-start | bytes 262144 | tf_op jit(solution)/shard_map/all_to_all | solution.py:146
  479.7 14.8 %all-to-all-start.6 = ((f32[32,8,128]{2,1,0:T(8,128)}), f32[32,8,128]{2,1,0:T(8,128)S(1)}, u32[]{:S(2)}, u32[]{:S(2)}) async-start(f32[32,8,128]{2,1,0:T(8,128)} %broadcast_in_dim.17), calls=%async_computation.6 | async-start | bytes 262144 | tf_op jit(solution)/shard_map/all_to_all | solution.py:149
Sparse Core Ops, SparseCore 0:
  398.4 33.9 all-gather.2
